TPU v7x, 32 devices: a whole 2x2x4 slice. The times are simulated.
32 devices in a mesh: dp: 4 (over x, core), fsdp: 8 (over z, y).
Axes of the slice: x: 2, y: 2, z: 4, core: 2. Of those that a mesh axis runs over, the one named last changes fastest.
Arguments:
- tokens: bfloat16 [64, 512, 768], P(('dp', 'fsdp')), may hold values from -6 to 6
- segment_ids: int32 [64, 512], P(('dp', 'fsdp')), may hold values from 0 to 32, as said below
- qkv_weight: bfloat16 [768, 576], P(('dp', 'fsdp')), may hold values from -0.4375 to 0.4375
- out_weight: bfloat16 [768, 768], P(('dp', 'fsdp')), may hold values from -2.5 to 2.5
- up_weight: bfloat16 [768, 768], P(('dp', 'fsdp')), may hold values from -0.4375 to 0.4375
- down_weight: bfloat16 [3072, 192], P(('dp', 'fsdp')), may hold values from -0.21875 to 0.21875
- biases: bfloat16 [6, 768], P(None, ('dp', 'fsdp')), may hold values from -1 to 1
- up_bias: bfloat16 [3072], P(('dp', 'fsdp')), may hold values from -2.5 to 2.5
- gains: bfloat16 [2, 768], P(None, ('dp', 'fsdp')), may hold values from 0.5 to 1.5
- cotangent: bfloat16 [64, 512, 768], P(('dp', 'fsdp')), may hold values from -6 to 6
Outputs:
- layer_out: bfloat16 [64, 512, 768], P(('dp', 'fsdp'))
- input_grad: float32 [64, 512, 768], P(('dp', 'fsdp'))
- qkv_grad: float32 [768, 576], P(('dp', 'fsdp'))
- out_grad: float32 [768, 768], P(('dp', 'fsdp'))
- up_grad: float32 [768, 768], P(('dp', 'fsdp'))
- down_grad: float32 [3072, 192], P(('dp', 'fsdp'))
- bias_grad: float32 [6, 768], P(None, ('dp', 'fsdp'))
- up_bias_grad: float32 [3072], P(('dp', 'fsdp'))
- gain_grad: float32 [2, 768], P(None, ('dp', 'fsdp'))
Inputs may be any that keep to these rules, and one draw needn't show every extreme that they name: `segment_ids`: in each row the real tokens carry document numbers from 1 upward that never fall, each document contiguous; after them come 0 to 64 padding tokens numbered 0, exactly 64 in the first row.
All inputs are finite; a program needn't handle non-finite values.
Results may differ from a plain program's by a relative error of at most 0.012.
The roundings to bfloat16 on the way count: a program that leaves them out, or rounds other values in their place, can miss the bound.
Values may be sent and summed in bfloat16 or wider, within the bound.
A program may use at most 128 MiB of HBM per device.

v0:
```python
from functools import partial
import jax
import jax.numpy as jnp
from jax import lax
from jax.sharding import PartitionSpec as P

HEADS = 12
GROUPS = 4
EPSILON = 1e-05
SCORE_SCALE = 0.125
NEG_FILL = -1e30


def group_apply(values, weight):
    parts = values.reshape(values.shape[0], GROUPS, -1)
    table = weight.reshape(GROUPS, parts.shape[2], -1)
    return jnp.einsum("ngc,gce->nge", parts, table, preferred_element_type=jnp.float32)


def normalize(hidden):
    centre = hidden - jnp.mean(hidden, -1, keepdims=True)
    spread = lax.rsqrt(jnp.mean(centre * centre, -1, keepdims=True) + EPSILON)
    return (centre * spread, spread)


def norm_back(upstream, gain, normed, spread):
    scaled = upstream * gain
    return spread * (
        scaled
        - jnp.mean(scaled, -1, keepdims=True)
        - normed * jnp.mean(scaled * normed, -1, keepdims=True)
    )


def block_scores(query_blk, keys_seq, seg_blk, seg_seq):
    raw = (
        jnp.einsum("qhd,khd->hqk", query_blk, keys_seq, preferred_element_type=jnp.float32)
        * SCORE_SCALE
    )
    allowed = (seg_seq != 0)[None, :] & (
        (seg_blk[:, None] == seg_seq[None, :]) | (seg_blk[:, None] == 0)
    )
    return jnp.where(allowed[None], raw, NEG_FILL)


def attend_forward(item):
    queries_s, keys_s, values_s, seg_s = item
    pieces, sums_log = ([], [])
    scores = block_scores(queries_s, keys_s, seg_s, seg_s)
    top = jnp.max(scores, -1, keepdims=True)
    expd = jnp.exp(scores - top)
    total = jnp.sum(expd, -1, keepdims=True)
    probs = (expd / total).astype(jnp.bfloat16)
    pieces.append(jnp.einsum("hqk,khd->qhd", probs, values_s, preferred_element_type=jnp.float32))
    sums_log.append((top + jnp.log(total))[..., 0])
    return (jnp.concatenate(pieces, 0), jnp.concatenate(sums_log, 1))


def attend_backward(item):
    queries_s, keys_s, values_s, seg_s, lse_s, grad_ctx_s = item
    length = queries_s.shape[0]
    block_rows = min(512, length)
    grad_keys = jnp.zeros(keys_s.shape, jnp.float32)
    grad_values = jnp.zeros(values_s.shape, jnp.float32)
    scores = block_scores(queries_s, keys_s, seg_s, seg_s)
    probs = jnp.exp(scores - lse_s[:, 0:block_rows, None])
    grad_values = grad_values + jnp.einsum(
        "hqk,qhd->khd", probs.astype(jnp.bfloat16), grad_ctx_s, preferred_element_type=jnp.float32
    )
    grad_probs = jnp.einsum(
        "qhd,khd->hqk", grad_ctx_s, values_s, preferred_element_type=jnp.float32
    )
    inner = jnp.sum(probs * grad_probs, -1, keepdims=True)
    grad_scores = (probs * (grad_probs - inner)).astype(jnp.bfloat16)
    query_parts = [
        jnp.einsum("hqk,khd->qhd", grad_scores, keys_s, preferred_element_type=jnp.float32)
        * SCORE_SCALE
    ]
    grad_keys = (
        grad_keys
        + jnp.einsum("hqk,qhd->khd", grad_scores, queries_s, preferred_element_type=jnp.float32)
        * SCORE_SCALE
    )
    return (jnp.concatenate(query_parts, 0), grad_keys, grad_values)


def reduce_ffn(up_grad, down_grad, up_bias_grad):
    return (
        lax.psum_scatter(up_grad, ("dp", "fsdp"), scatter_dimension=0, tiled=True),
        lax.psum_scatter(down_grad, ("dp", "fsdp"), scatter_dimension=0, tiled=True),
        lax.psum_scatter(up_bias_grad, ("dp", "fsdp"), scatter_dimension=0, tiled=True),
    )


def local(
    tokens,
    segment_ids,
    qkv_weight,
    out_weight,
    up_weight,
    down_weight,
    biases,
    up_bias,
    gains,
    cotangent,
):

    def fetch_attention():
        return (
            lax.all_gather(qkv_weight, ("dp", "fsdp"), axis=0, tiled=True),
            lax.all_gather(out_weight, ("dp", "fsdp"), axis=0, tiled=True),
            lax.all_gather(biases, ("dp", "fsdp"), axis=1, tiled=True),
            lax.all_gather(gains, ("dp", "fsdp"), axis=1, tiled=True),
        )

    def fetch_ffn():
        return (
            lax.all_gather(up_weight, ("dp", "fsdp"), axis=0, tiled=True),
            lax.all_gather(down_weight, ("dp", "fsdp"), axis=0, tiled=True),
            lax.all_gather(up_bias, ("dp", "fsdp"), axis=0, tiled=True),
        )

    qkv_full, out_full, bias_full, gain_full = fetch_attention()
    up_full, down_full, up_bias_full = fetch_ffn()
    count, length, width = tokens.shape
    rows = count * length
    group_w = width // GROUPS
    shape4 = (count, length, HEADS, width // HEADS)
    inputs = tokens.reshape(rows, width)
    bias_vals = bias_full.astype(jnp.float32)
    gain_vals = gain_full.astype(jnp.float32)
    mixed = group_apply(inputs, qkv_full)
    queries = (
        (mixed[:, :, :group_w].reshape(rows, width) + bias_vals[0])
        .astype(jnp.bfloat16)
        .reshape(shape4)
    )
    keys_all = (
        mixed[:, :, group_w : 2 * group_w].reshape(rows, width).astype(jnp.bfloat16).reshape(shape4)
    )
    values_all = (
        (mixed[:, :, 2 * group_w :].reshape(rows, width) + bias_vals[1])
        .astype(jnp.bfloat16)
        .reshape(shape4)
    )
    attended, lse = lax.map(attend_forward, (queries, keys_all, values_all, segment_ids))
    context = attended.reshape(rows, width).astype(jnp.bfloat16)
    hidden1 = (
        inputs.astype(jnp.float32)
        + jnp.dot(context, out_full, preferred_element_type=jnp.float32)
        + bias_vals[2]
    )
    normed1, spread1 = normalize(hidden1)
    layer1 = normed1 * gain_vals[0] + bias_vals[3]
    layer1_low = layer1.astype(jnp.bfloat16)
    pre_act = group_apply(layer1_low, up_full).reshape(rows, -1) + up_bias_full.astype(jnp.float32)
    activ, gelu_pull = jax.vjp(partial(jax.nn.gelu, approximate=False), pre_act)
    activ_low = activ.astype(jnp.bfloat16)
    hidden2 = layer1 + group_apply(activ_low, down_full).reshape(rows, width) + bias_vals[4]
    normed2, spread2 = normalize(hidden2)
    layer_out = (
        (normed2 * gain_vals[1] + bias_vals[5]).astype(jnp.bfloat16).reshape(count, length, width)
    )
    qkv_back, out_back, unused_bias, gain_back = fetch_attention()
    up_back, down_back, unused_up = fetch_ffn()
    gain_back = gain_back.astype(jnp.float32)
    grad_out = cotangent.reshape(rows, width).astype(jnp.float32)
    grad_h2 = norm_back(grad_out, gain_back[1], normed2, spread2)
    grad_f_low = grad_h2.astype(jnp.bfloat16).reshape(rows, GROUPS, group_w)
    down_grad = jnp.einsum(
        "lut,lux->utx",
        activ_low.reshape(rows, GROUPS, -1),
        grad_f_low,
        preferred_element_type=jnp.float32,
    ).reshape(-1, group_w)
    grad_act = jnp.einsum(
        "ipo,pso->ips",
        grad_f_low,
        down_back.reshape(GROUPS, -1, group_w),
        preferred_element_type=jnp.float32,
    ).reshape(rows, -1)
    grad_pre = gelu_pull(grad_act)[0].astype(jnp.bfloat16)
    up_bias_grad = jnp.sum(grad_pre, 0, dtype=jnp.float32)
    grad_pre_groups = grad_pre.reshape(rows, GROUPS, -1)
    up_grad = jnp.einsum(
        "ngc,ngf->gcf",
        layer1_low.reshape(rows, GROUPS, group_w),
        grad_pre_groups,
        preferred_element_type=jnp.float32,
    ).reshape(width, -1)
    grad_l1 = grad_h2 + jnp.einsum(
        "ngf,gcf->ngc",
        grad_pre_groups,
        up_back.reshape(GROUPS, group_w, -1),
        preferred_element_type=jnp.float32,
    ).reshape(rows, width)
    grad_h1 = norm_back(grad_l1, gain_back[0], normed1, spread1)
    grad_attn = grad_h1.astype(jnp.bfloat16)
    out_grad = jnp.einsum("nc,ne->ce", context, grad_attn, preferred_element_type=jnp.float32)
    grad_ctx = jnp.einsum(
        "ne,ce->nc", grad_attn, out_back, preferred_element_type=jnp.float32
    ).astype(jnp.bfloat16)
    grad_queries, grad_keys, grad_values = lax.map(
        attend_backward, (queries, keys_all, values_all, segment_ids, lse, grad_ctx.reshape(shape4))
    )
    grad_q = grad_queries.reshape(rows, width).astype(jnp.bfloat16)
    grad_k = grad_keys.reshape(rows, width).astype(jnp.bfloat16)
    grad_v = grad_values.reshape(rows, width).astype(jnp.bfloat16)
    grad_mixed = jnp.concatenate(
        [
            grad_q.reshape(rows, GROUPS, group_w),
            grad_k.reshape(rows, GROUPS, group_w),
            grad_v.reshape(rows, GROUPS, group_w),
        ],
        -1,
    )
    qkv_grad = jnp.einsum(
        "ngc,nge->gce",
        inputs.reshape(rows, GROUPS, group_w),
        grad_mixed,
        preferred_element_type=jnp.float32,
    ).reshape(width, -1)
    input_grad = grad_h1 + jnp.einsum(
        "nge,gce->ngc",
        grad_mixed,
        qkv_back.reshape(GROUPS, group_w, -1),
        preferred_element_type=jnp.float32,
    ).reshape(rows, width)
    bias_grad = jnp.stack(
        [
            jnp.sum(grad_q, 0, dtype=jnp.float32),
            jnp.sum(grad_v, 0, dtype=jnp.float32),
            jnp.sum(grad_h1, 0),
            jnp.sum(grad_l1, 0),
            jnp.sum(grad_h2, 0),
            jnp.sum(grad_out, 0),
        ]
    )
    gain_grad = jnp.stack([jnp.sum(grad_l1 * normed1, 0), jnp.sum(grad_out * normed2, 0)])
    qkv_sum, out_sum, bias_sum, gain_sum = (
        lax.psum_scatter(qkv_grad, ("dp", "fsdp"), scatter_dimension=0, tiled=True),
        lax.psum_scatter(out_grad, ("dp", "fsdp"), scatter_dimension=0, tiled=True),
        lax.psum_scatter(bias_grad, ("dp", "fsdp"), scatter_dimension=1, tiled=True),
        lax.psum_scatter(gain_grad, ("dp", "fsdp"), scatter_dimension=1, tiled=True),
    )
    ffn_sums = reduce_ffn(up_grad, down_grad, up_bias_grad)
    up_sum, down_sum, up_bias_sum = ffn_sums
    return (
        layer_out,
        input_grad.reshape(count, length, width),
        qkv_sum,
        out_sum,
        up_sum,
        down_sum,
        bias_sum,
        up_bias_sum,
        gain_sum,
    )


def solution(mesh):
    in_specs = (
        P(("dp", "fsdp"), None, None),
        P(("dp", "fsdp"), None),
        P(("dp", "fsdp"), None),
        P(("dp", "fsdp"), None),
        P(("dp", "fsdp"), None),
        P(("dp", "fsdp"), None),
        P(None, ("dp", "fsdp")),
        P(("dp", "fsdp")),
        P(None, ("dp", "fsdp")),
        P(("dp", "fsdp"), None, None),
    )
    out_specs = (
        P(("dp", "fsdp"), None, None),
        P(("dp", "fsdp"), None, None),
        P(("dp", "fsdp"), None),
        P(("dp", "fsdp"), None),
        P(("dp", "fsdp"), None),
        P(("dp", "fsdp"), None),
        P(None, ("dp", "fsdp")),
        P(("dp", "fsdp")),
        P(None, ("dp", "fsdp")),
    )
    return jax.shard_map(local, mesh=mesh, in_specs=in_specs, out_specs=out_specs, check_vma=False)
```

profile of v0, /device:TPU:0, one launch (start us, length us, event | category | flops | bytes accessed | tf_op | source)
XLA Modules:
  0.0 926.9 jit_solution(14447026839796752932)
XLA Ops:
  9.5 4.9 copy.94
  16.0 81.7 %all_gather.26 = bf16[768,576]{1,0:T(8,128)(2,1)} all-gather(bf16[24,576]{1,0:T(8,128)(2,1)S(1)} %copy-done.27), channel_id=1, replica_groups=mesh['dp'=4,'fsdp'=8] {'dp','fsdp'}, dimensions={0}, use_global_device_ids=true | all-gather | bytes 912384 | tf_op jit(solution)/shard_map/all_gather | solution.py:110
  97.7 3.8 reshape_reshape.4
  101.5 3.2 convolution_bitcast_fusion
  106.0 3.4 fusion.77
  109.6 37.1 %all-reduce = bf16[3072]{0:T(1024)(128)(2,1)S(1)} all-reduce(bf16[3072]{0:T(1024)(128)(2,1)S(1)} %dynamic-update-slice), channel_id=1, replica_groups=mesh['dp'=4,'fsdp'=8] {'dp','fsdp'}, use_global_device_ids=true, to_apply=%add | all-reduce | flops 3072 | bytes 12288
  146.7 65.6 %all-gather.1 = bf16[32,24,2]{1,2,0:T(2,128)(2,1)S(1)} all-gather(bf16[1,24,2]{1,2,0:T(2,128)(2,1)S(1)} %bitcast.304), channel_id=1, replica_groups=mesh['dp'=4,'fsdp'=8] {'dp','fsdp'}, dimensions={0}, use_global_device_ids=true | all-gather | bytes 3168 | tf_op jit(solution)/shard_map/all_gather | solution.py:113
  212.6 2.7 convert_reduce_fusion.3
  216.0 63.9 %all-gather = bf16[32,24,6]{1,2,0:T(8,128)(2,1)S(1)} all-gather(bf16[1,24,6]{1,2,0:T(8,128)(2,1)S(1)} %bitcast.303), channel_id=1, replica_groups=mesh['dp'=4,'fsdp'=8] {'dp','fsdp'}, dimensions={0}, use_global_device_ids=true | all-gather | bytes 9504 | tf_op jit(solution)/shard_map/all_gather | solution.py:112
  280.9 3.1 copy.125
  284.0 2.4 copy.121
  286.3 5.7 reshape.348
  292.0 2.3 convert_element_type.116
  294.4 1.7 copy.99
  296.1 5.7 reshape.347
  301.8 5.0 fusion.66
  308.1 21.2 %while.26 = (s32[]{:T(128)}, bf16[2,512,12,64]{1,3,2,0:T(8,128)(2,1)}, f32[2,12,512]{2,1,0:T(8,128)S(1)}, bf16[2,512,12,64]{1,3,2,0:T(8,128)(2,1)}, s32[2,512]{1...) while((s32[]{:T(128)}, ...), condition=%wide.region_3.4_spmd, body=%wide.region_0.3_spmd.sunk | while | flops 843836416 | bytes 42963044 | solution.py:146
  308.4 2.1 fusion.122
  310.5 2.6 fusion.123
  313.1 5.5 bitcast_dynamic-update-slice_fusion.10
  318.9 2.1 fusion.122
  321.0 2.6 fusion.123
  323.6 5.5 bitcast_dynamic-update-slice_fusion.10
  329.3 3.0 copy.100
  333.9 4.3 fusion.78
  341.6 33.3 %fusion.52 = (bf16[1024,4,768]{2,0,1:T(8,128)(2,1)}, f32[1024,4,768]{2,0,1:T(8,128)}, f32[4,1024,768]{2,1,0:T(8,128)}) fusion(f32[4,768]{1,0:T(4,128)S(1)} %reshape.363, bf16[1024,4,192]{0,2,1:T(8,128)(2,1)} %bitcast.281, bf16[4,192,768]{2,1,0:T(8,128)(2,1)} %bitcast.294), kind=kOutput, calls=%fused_computation.77 | convolution fusion | flops 1415577600 | bytes 34222080 | tf_op jit(solution)/shard_map/ngc,gce->nge/dot_general | solution.py:17
  374.9 5.6 fusion.79
  384.8 3.1 fusion.72
  390.5 15.7 %convert_reduce_fusion = (f32[4,768]{1,0:T(4,128)}, bf16[1024,4,768]{2,0,1:T(8,128)(2,1)}) fusion(f32[1024,4,768]{2,0,1:T(8,128)} %get-tuple-element.275, bf16[1024,4,192]{0,2,1:T(8,128)(2,1)S(1)} %bitcast.285, bf16[4,768,192]{2,1,0:T(8,128)(2,1)S(1)} %bitcast.293, f32[4,1024,768]{2,1,0:T(8,128)} %get-tuple-element.285, f32[4,768]{1,0:T(4,128)S(1)} %reshape.363), kind=kOutput, calls=%fused_computation.78 | convolution fusion | flops 1261433856 | bytes 34234368 | tf_op jit(solution)/shard_map/ipo,pso->ips/dot_general | solution.py:176
  406.2 5.1 fusion.80
  411.3 2.2 multiply_reduce_fusion.2
  413.6 1.7 fusion.73
  417.0 2.6 convolution_convert_fusion
  419.6 2.6 copy.107
  422.2 3.9 reshape.356
  426.0 2.9 copy.109
  433.0 49.2 %while.27 = (s32[]{:T(128)}, bf16[2,512,12,64]{1,3,2,0:T(8,128)(2,1)}, bf16[2,512,12,64]{1,3,2,0:T(8,128)(2,1)}, bf16[2,512,12,64]{1,3,2,0:T(8,128)(2,1)}, bf16[...) while((s32[]{:T(128)}, ...), condition=%wide.region_14.15_spmd, body=%wide.region_12.14_spmd.sunk | while | flops 2062019584 | bytes 143596848 | solution.py:203
  433.5 1.8 fusion.132
  435.4 3.9 bitcast_dynamic-update-slice_fusion.14
  439.3 6.9 multiply_reduce_fusion.10
  446.2 7.1 multiply_convert_fusion.2
  453.3 2.0 bitcast_dynamic-update-slice_fusion.13
  458.0 1.8 fusion.132
  459.9 3.9 bitcast_dynamic-update-slice_fusion.14
  463.8 6.9 multiply_reduce_fusion.10
  470.7 7.1 multiply_convert_fusion.2
  477.8 2.0 bitcast_dynamic-update-slice_fusion.13
  482.1 3.0 copy.111
  486.6 4.3 copy.112
  490.9 3.8 convert_element_type.135
  494.7 2.8 copy.110
  497.5 3.8 convert_element_type.131
  504.4 3.2 fusion.81
  507.7 6.7 fusion.84
  515.8 5.7 fusion.82
  521.7 5.2 fusion.69
  527.0 2.9 copy.124
  532.1 3.9 fusion.83
  536.8 2.4 copy.127
  539.2 39.6 %all-reduce.5 = (f32[6,768]{1,0:T(8,128)S(1)}, f32[3072]{0:T(1024)S(1)}, f32[2,768]{1,0:T(2,128)S(1)}) all-reduce(f32[6,768]{1,0:T(8,128)S(1)} %stack.36, f32[3072]{0:T(1024)S(1)} %reduce_sum.188, f32[2,768]{1,0:T(2,128)S(1)} %pad_maximum_fusion), channel_id=6, replica_groups=mesh['dp'=4,'fsdp'=8] {'dp','fsdp'}, use_global_device_ids=true, to_apply=%region_25.26.clone | all-reduce | flops 9216 | bytes 73728
  580.7 24.0 %reduce-scatter.17.cloned.1.call-done = f32[24,576]{1,0:T(8,128)} async-done(((f32[768,576]{1,0:T(8,128)}), f32[24,576]{1,0:T(8,128)}) %reduce-scatter.17.cloned.1.call-update) | async-done | bytes 55312
  604.7 106.4 %reduce-scatter.15.cloned.1.call-done = f32[96,192]{1,0:T(8,128)} async-done(((f32[3072,192]{1,0:T(8,128)}), f32[96,192]{1,0:T(8,128)}) %reduce-scatter.15.cloned.1.call-update) | async-done | bytes 73744
  711.1 103.7 %reduce-scatter.13.cloned.1.call-done = f32[24,768]{1,0:T(8,128)} async-done(((f32[768,768]{1,0:T(8,128)}), f32[24,768]{1,0:T(8,128)}) %reduce-scatter.13.cloned.1.call-update) | async-done | bytes 73744 | tf_op jit(solution)/shard_map/reduce_scatter | solution.py:89
  814.8 104.8 %reduce-scatter.11.cloned.1.call-done = f32[24,768]{1,0:T(8,128)} async-done(((f32[768,768]{1,0:T(8,128)}), f32[24,768]{1,0:T(8,128)}) %reduce-scatter.11.cloned.1.call-update) | async-done | bytes 73744 | tf_op jit(solution)/shard_map/reduce_scatter | solution.py:242
  (188 shorter events, 42.9 us)
Async XLA Ops:
  7.2 326.7 %all-gather.6.cloned.1.call-start = ((), (), s32[]{:S(2)}) async-start(), calls=%async_computation.4 | async-start | bytes 1216512 | tf_op jit(solution)/shard_map/all_gather | solution.py:111
  7.9 333.6 %all-gather.8.cloned.1.call-start = ((), (), s32[]{:S(2)}) async-start(), calls=%async_computation.5 | async-start | bytes 1216512 | tf_op jit(solution)/shard_map/all_gather | solution.py:118
  8.7 366.2 %all-gather.10.cloned.1.call-start = ((), (), s32[]{:S(2)}) async-start(), calls=%async_computation.6 | async-start | bytes 1622016 | tf_op jit(solution)/shard_map/all_gather | solution.py:119
  9.4 595.3 %reduce-scatter.17.cloned.1.call-start = ((), (), s32[]{:S(2)}) async-start(), calls=%async_computation.10 | async-start | bytes 2027520
  14.4 1.7 copy-start.27
  106.0 3.4 copy-start.41
  106.0 40.7 %copy-start.39 = (bf16[2,24]{1,0:T(2,128)(2,1)S(1)}, bf16[2,24]{1,0:T(2,128)(2,1)}, u32[]{:S(2)}) copy-start(bf16[2,24]{1,0:T(2,128)(2,1)} %param.22) | copy-start | bytes 292
  106.0 109.9 %copy-start.38 = (bf16[6,24]{1,0:T(8,128)(2,1)S(1)}, bf16[6,24]{1,0:T(8,128)(2,1)}, u32[]{:S(2)}) copy-start(bf16[6,24]{1,0:T(8,128)(2,1)} %param.20) | copy-start | bytes 868
  212.6 3.3 copy-start.25
  286.3 5.7 copy-start.16
  301.8 6.3 copy-start.24
  338.3 1.6 copy-start
  374.9 5.6 copy-start.1
  374.9 5.6 copy-start.35
  381.3 1.9 copy-start.2
  381.3 1.9 copy-start.26
  383.2 1.6 copy-start.33
  383.2 1.6 copy-start.34
  387.9 1.7 copy-start.3
  387.9 2.5 copy-start.22
  389.8 16.4 %copy-start.20 = (bf16[1024,768]{0,1:T(8,128)(2,1)}, bf16[1024,768]{0,1:T(8,128)(2,1)S(1)}, u32[]{:S(2)}) copy-start(bf16[1024,768]{0,1:T(8,128)(2,1)S(1)} %convert_element_type.126) | copy-start | bytes 4718596
  390.5 15.7 %copy-start.23 = (bf16[768,768]{1,0:T(8,128)(2,1)S(1)}, bf16[768,768]{1,0:T(8,128)(2,1)}, u32[]{:S(2)}) copy-start(bf16[768,768]{1,0:T(8,128)(2,1)} %all-gather.8.cloned.1.call-done) | copy-start | bytes 3538948
  406.2 5.1 copy-start.4
  413.6 3.4 copy-start.40
  415.3 1.7 copy-start.10
  433.5 1.9 copy-start.6
  435.4 4.0 copy-start.5
  446.2 7.1 copy-start.17
  453.3 2.0 copy-start.7
  455.4 1.2 copy-start.18
  456.5 1.1 copy-start.8
  458.0 1.9 copy-start.6
  459.9 4.0 copy-start.5
  470.7 7.1 copy-start.17
  477.8 2.0 copy-start.7
  479.8 1.2 copy-start.18
  481.0 1.1 copy-start.8
  486.6 8.1 copy-start.9
  501.3 1.9 copy-start.19
  502.9 1.5 copy-start.13
  504.4 3.2 copy-start.14
  504.4 3.3 copy-start.21
  507.6 203.5 %reduce-scatter.15.cloned.1.call-start = ((), (), s32[]{:S(2)}) async-start(), calls=%async_computation.9 | async-start | bytes 3244032
  514.4 1.4 copy-start.15
  514.4 300.3 %reduce-scatter.13.cloned.1.call-start = ((), (), s32[]{:S(2)}) async-start(), calls=%async_computation.8 | async-start | bytes 2433024 | tf_op jit(solution)/shard_map/reduce_scatter | solution.py:89
  521.6 5.3 copy-start.30
  521.6 5.4 copy-start.36
  521.6 5.4 copy-start.31
  521.6 397.9 %reduce-scatter.11.cloned.1.call-start = ((), (), s32[]{:S(2)}) async-start(), calls=%async_computation.7 | async-start | bytes 2433024 | tf_op jit(solution)/shard_map/reduce_scatter | solution.py:242
  526.9 3.0 copy-start.37
  526.9 3.0 copy-start.29
  526.9 3.0 copy-start.28
  526.9 3.1 copy-start.32
  527.0 5.1 copy-start.12
  532.1 3.9 copy-start.11
Sparse Core Ops, SparseCore 0:
  10.9 57.2 all-gather.5
  71.1 53.4 all-gather.7
  127.5 53.8 all-gather.9
  507.8 96.8 reduce-scatter.16
  610.5 100.5 reduce-scatter.14
  716.8 97.9 reduce-scatter.12
  821.5 98.0 reduce-scatter.10
where the time goes:
time: 933 us; the launch traced here: 927 us
  waiting for transfers between devices  341 us (37%)
  blocking collectives  288 us (31%)
  matrix products  141 us (15%)
  local copies, waits for them, and re-layouts  95.8 us (10%)
  other arithmetic  44.8 us (5%)
  between operations  15.1 us (2%)
    unnamed x9, waiting for transfers between devices  133 us
    reduce_scatter x1, waiting for transfers between devices, local(): lax.psum_scatter(out_grad, ('dp', 'fsdp'), scatter_dimension=0, tiled=True)  105 us
    reduce_scatter x1, waiting for transfers between devices, reduce_ffn(): lax.psum_scatter(up_grad, ('dp', 'fsdp'), scatter_dimension=0, tiled=True)  104 us
    all_gather x1, blocking collectives, fetch_attention(): lax.all_gather(qkv_weight, ('dp', 'fsdp'), axis=0, tiled=True)  81.7 us
    unnamed x2, blocking collectives  76.7 us
    all_gather x1, blocking collectives, fetch_attention(): lax.all_gather(gains, ('dp', 'fsdp'), axis=1, tiled=True)  65.6 us
    all_gather x1, blocking collectives, fetch_attention(): lax.all_gather(biases, ('dp', 'fsdp'), axis=1, tiled=True)  63.9 us
    dot_general x3, matrix products, group_apply(): jnp.einsum('ngc,gce->nge', parts, table, preferred_element_type=jnp.float32)  42 us
  transfers between devices with their start and end apart: 7, of which 4 were waited for; matrix products, arithmetic and copies ran while one was open for 16% of the time, Pallas kernels for 0%

commit v1 on v0

--- a/solution.py
+++ b/solution.py
@@ -9,6 +9,18 @@
 EPSILON = 1e-05
 SCORE_SCALE = 0.125
 NEG_FILL = -1e30
+
+
+def gather_by_bits(array, axis, dim):
+    ways, here, step = (lax.axis_size(axis), lax.axis_index(axis), array.shape[dim])
+    line, have = (array, 1)
+    while have < ways:
+        line = jnp.concatenate(
+            [line, lax.ppermute(line, axis, [(d, (d - have) % ways) for d in range(ways)])],
+            axis=dim,
+        )
+        have = 2 * have
+    return jnp.roll(line, here * step, axis=dim)
 
 
 def group_apply(values, weight):
@@ -107,7 +119,7 @@
 
     def fetch_attention():
         return (
-            lax.all_gather(qkv_weight, ("dp", "fsdp"), axis=0, tiled=True),
+            gather_by_bits(qkv_weight, ("dp", "fsdp"), 0),
             lax.all_gather(out_weight, ("dp", "fsdp"), axis=0, tiled=True),
             lax.all_gather(biases, ("dp", "fsdp"), axis=1, tiled=True),
             lax.all_gather(gains, ("dp", "fsdp"), axis=1, tiled=True),

time: 933 us -> 870 us (0.932)
  blocking collectives: 288 us -> 209 us
    all_gather x1 -> x0, blocking collectives: 81.7 us -> none  [fetch_attention(): lax.all_gather(qkv_weight, ('dp', 'fsdp'), axis=0, tiled=True)]
    unnamed x84 -> x92, local copies, waits for them, and re-layouts: 25.5 us -> 28.3 us
  transfers between devices with their start and end apart: 7 -> 12, of which waited for: 4 -> 6; matrix products, arithmetic and copies ran while one was open for 16% -> 17% of each run, Pallas kernels for 0% -> 0%
where the time goes in v1:
time: 870 us; the launch traced here: 866 us
  waiting for transfers between devices  348 us (40%)
  blocking collectives  209 us (24%)
  matrix products  140 us (16%)
  local copies, waits for them, and re-layouts  96.1 us (11%)
  other arithmetic  49.4 us (6%)
  between operations  15 us (2%)
    unnamed x9, waiting for transfers between devices  132 us
    reduce_scatter x1, waiting for transfers between devices, local(): lax.psum_scatter(out_grad, ('dp', 'fsdp'), scatter_dimension=0, tiled=True)  105 us
    reduce_scatter x1, waiting for transfers between devices, reduce_ffn(): lax.psum_scatter(up_grad, ('dp', 'fsdp'), scatter_dimension=0, tiled=True)  104 us
    unnamed x2, blocking collectives  79 us
    all_gather x1, blocking collectives, fetch_attention(): lax.all_gather(biases, ('dp', 'fsdp'), axis=1, tiled=True)  66.2 us
    all_gather x1, blocking collectives, fetch_attention(): lax.all_gather(gains, ('dp', 'fsdp'), axis=1, tiled=True)  63.7 us
    dot_general x3, matrix products, group_apply(): jnp.einsum('ngc,gce->nge', parts, table, preferred_element_type=jnp.float32)  40.3 us
    unnamed x92, local copies, waits for them, and re-layouts  28.3 us
  transfers between devices with their start and end apart: 12, of which 6 were waited for; matrix products, arithmetic and copies ran while one was open for 17% of the time, Pallas kernels for 0%

profile of v1, /device:TPU:0, one launch (start us, length us, event | category | flops | bytes accessed | tf_op | source)
XLA Modules:
  0.0 866.0 jit_solution(471273390161614439)
XLA Ops:
  8.7 6.4 collective-permute-start
  15.2 63.7 %all-gather.1 = bf16[32,24,2]{1,2,0:T(2,128)(2,1)S(1)} all-gather(bf16[1,24,2]{1,2,0:T(2,128)(2,1)} %bitcast.304), channel_id=1, replica_groups=mesh['dp'=4,'fsdp'=8] {'dp','fsdp'}, dimensions={0}, use_global_device_ids=true | all-gather | bytes 3168 | tf_op jit(solution)/shard_map/all_gather | solution.py:125
  79.8 2.7 convert_reduce_fusion.3
  85.6 40.2 %all-reduce = bf16[3072]{0:T(1024)(128)(2,1)S(1)} all-reduce(bf16[3072]{0:T(1024)(128)(2,1)S(1)} %dynamic-update-slice), channel_id=1, replica_groups=mesh['dp'=4,'fsdp'=8] {'dp','fsdp'}, use_global_device_ids=true, to_apply=%add | all-reduce | flops 3072 | bytes 12288
  126.9 66.2 %all-gather = bf16[32,24,6]{1,2,0:T(8,128)(2,1)S(1)} all-gather(bf16[1,24,6]{1,2,0:T(8,128)(2,1)} %bitcast.303), channel_id=1, replica_groups=mesh['dp'=4,'fsdp'=8] {'dp','fsdp'}, dimensions={0}, use_global_device_ids=true | all-gather | bytes 9504 | tf_op jit(solution)/shard_map/all_gather | solution.py:124
  195.0 5.1 collective-permute-done.2
  202.4 2.4 collective-permute-done.3
  207.9 3.8 copy.94
  211.7 2.3 reshape_reshape.4
  214.0 2.1 copy.125
  217.8 2.4 copy.121
  220.2 2.0 constant_dynamic-update-slice_fusion.5
  222.1 2.2 fusion.69
  227.2 2.2 fusion.78
  229.4 3.8 reshape.348
  233.2 2.9 convert_element_type.116
  236.4 5.7 reshape.347
  242.1 5.0 fusion.66
  248.4 21.1 %while.26 = (s32[]{:T(128)}, bf16[2,512,12,64]{1,3,2,0:T(8,128)(2,1)}, f32[2,12,512]{2,1,0:T(8,128)S(1)}, bf16[2,512,12,64]{1,3,2,0:T(8,128)(2,1)}, s32[2,512]{1...) while((s32[]{:T(128)}, ...), condition=%wide.region_3.5_spmd, body=%wide.region_0.4_spmd.sunk | while | flops 843836416 | bytes 42963044 | solution.py:158
  248.9 2.1 fusion.123
  251.0 2.6 fusion.124
  253.6 5.5 bitcast_dynamic-update-slice_fusion.10
  259.4 2.1 fusion.123
  261.5 2.6 fusion.124
  264.0 5.5 bitcast_dynamic-update-slice_fusion.10
  269.5 3.0 copy.100
  274.1 4.3 fusion.79
  281.8 33.3 %fusion.52 = (bf16[1024,4,768]{2,0,1:T(8,128)(2,1)}, f32[1024,4,768]{2,0,1:T(8,128)}, f32[4,1024,768]{2,1,0:T(8,128)}) fusion(f32[4,768]{1,0:T(4,128)S(1)} %copy-done.41, bf16[1024,4,192]{0,2,1:T(8,128)(2,1)} %bitcast.281, bf16[4,192,768]{2,1,0:T(8,128)(2,1)} %bitcast.294), kind=kOutput, calls=%fused_computation.77 | convolution fusion | flops 1415577600 | bytes 34222080 | tf_op jit(solution)/shard_map/ngc,gce->nge/dot_general | solution.py:29
  315.1 5.6 fusion.80
  325.0 3.2 fusion.73
  330.7 15.7 %convert_reduce_fusion = (f32[4,768]{1,0:T(4,128)}, bf16[1024,4,768]{2,0,1:T(8,128)(2,1)}) fusion(f32[1024,4,768]{2,0,1:T(8,128)} %get-tuple-element.276, bf16[1024,4,192]{0,2,1:T(8,128)(2,1)S(1)} %bitcast.285, bf16[4,768,192]{2,1,0:T(8,128)(2,1)S(1)} %bitcast.293, f32[4,1024,768]{2,1,0:T(8,128)} %get-tuple-element.296, f32[4,768]{1,0:T(4,128)S(1)} %copy-done.41), kind=kOutput, calls=%fused_computation.78 | convolution fusion | flops 1261433856 | bytes 34234368 | tf_op jit(solution)/shard_map/ipo,pso->ips/dot_general | solution.py:188
  346.4 5.1 fusion.81
  351.5 2.2 multiply_reduce_fusion.2
  357.2 2.6 convolution_convert_fusion
  359.8 2.6 copy.107
  362.4 3.9 reshape.356
  366.2 2.9 copy.109
  373.2 49.2 %while.27 = (s32[]{:T(128)}, bf16[2,512,12,64]{1,3,2,0:T(8,128)(2,1)}, bf16[2,512,12,64]{1,3,2,0:T(8,128)(2,1)}, bf16[2,512,12,64]{1,3,2,0:T(8,128)(2,1)}, bf16[...) while((s32[]{:T(128)}, ...), condition=%wide.region_14.16_spmd, body=%wide.region_12.15_spmd.sunk | while | flops 2062019584 | bytes 143596848 | solution.py:215
  373.7 1.8 fusion.133
  375.6 3.9 bitcast_dynamic-update-slice_fusion.14
  379.5 6.9 multiply_reduce_fusion.10
  386.4 7.1 multiply_convert_fusion.2
  393.5 2.0 bitcast_dynamic-update-slice_fusion.13
  400.1 3.9 bitcast_dynamic-update-slice_fusion.14
  404.0 6.9 multiply_reduce_fusion.10
  410.9 7.1 multiply_convert_fusion.2
  418.0 2.0 bitcast_dynamic-update-slice_fusion.13
  422.3 3.0 copy.111
  426.8 4.3 copy.112
  431.1 3.8 convert_element_type.135
  434.9 2.8 copy.110
  437.7 3.8 convert_element_type.131
  444.6 3.2 fusion.83
  447.9 6.7 fusion.85
  456.0 5.7 fusion.84
  461.9 5.2 fusion.70
  467.2 2.9 copy.124
  472.3 3.9 fusion.82
  477.0 2.4 copy.127
  479.4 38.9 %all-reduce.5 = (f32[6,768]{1,0:T(8,128)S(1)}, f32[3072]{0:T(1024)S(1)}, f32[2,768]{1,0:T(2,128)S(1)}) all-reduce(f32[6,768]{1,0:T(8,128)S(1)} %stack.36, f32[3072]{0:T(1024)S(1)} %reduce_sum.188, f32[2,768]{1,0:T(2,128)S(1)} %pad_maximum_fusion.3), channel_id=6, replica_groups=mesh['dp'=4,'fsdp'=8] {'dp','fsdp'}, use_global_device_ids=true, to_apply=%region_25.27.clone | all-reduce | flops 9216 | bytes 73728
  520.2 23.7 %reduce-scatter.17.cloned.1.call-done = f32[24,576]{1,0:T(8,128)} async-done(((f32[768,576]{1,0:T(8,128)}), f32[24,576]{1,0:T(8,128)}) %reduce-scatter.17.cloned.1.call-update) | async-done | bytes 55312
  543.9 106.5 %reduce-scatter.15.cloned.1.call-done = f32[96,192]{1,0:T(8,128)} async-done(((f32[3072,192]{1,0:T(8,128)}), f32[96,192]{1,0:T(8,128)}) %reduce-scatter.15.cloned.1.call-update) | async-done | bytes 73744
  650.4 103.7 %reduce-scatter.13.cloned.1.call-done = f32[24,768]{1,0:T(8,128)} async-done(((f32[768,768]{1,0:T(8,128)}), f32[24,768]{1,0:T(8,128)}) %reduce-scatter.13.cloned.1.call-update) | async-done | bytes 73744 | tf_op jit(solution)/shard_map/reduce_scatter | solution.py:101
  754.1 104.7 %reduce-scatter.11.cloned.1.call-done = f32[24,768]{1,0:T(8,128)} async-done(((f32[768,768]{1,0:T(8,128)}), f32[24,768]{1,0:T(8,128)}) %reduce-scatter.11.cloned.1.call-update) | async-done | bytes 73744 | tf_op jit(solution)/shard_map/reduce_scatter | solution.py:254
  (211 shorter events, 57.6 us)
Async XLA Ops:
  7.2 267.0 %all-gather.6.cloned.1.call-start = ((), (), s32[]{:S(2)}) async-start(), calls=%async_computation.4 | async-start | bytes 1216512 | tf_op jit(solution)/shard_map/all_gather | solution.py:123
  7.9 273.9 %all-gather.8.cloned.1.call-start = ((), (), s32[]{:S(2)}) async-start(), calls=%async_computation.5 | async-start | bytes 1216512 | tf_op jit(solution)/shard_map/all_gather | solution.py:130
  8.7 306.4 %all-gather.10.cloned.1.call-start = ((), (), s32[]{:S(2)}) async-start(), calls=%async_computation.6 | async-start | bytes 1622016 | tf_op jit(solution)/shard_map/all_gather | solution.py:131
  8.7 73.8 %collective-permute-start = (bf16[24,576]{1,0:T(8,128)(2,1)}, bf16[24,576]{1,0:T(8,128)(2,1)S(1)}, u32[]{:S(2)}, u32[]{:S(2)}) collective-permute-start(bf16[24,576]{1,0:T(8,128)(2,1)} %param.18), channel_id=1, source_target_pairs={{0,31},{1,0},{2,1},{3,2},{4,3},{5,4},{6,5},{7,6},{8,7},{9,8},{10,9... | collective-permute-start | bytes 82952 | tf_op jit(solution)/shard_map/ppermute | solution.py:19
  15.2 528.8 %reduce-scatter.17.cloned.1.call-start = ((), (), s32[]{:S(2)}) async-start(), calls=%async_computation.10 | async-start | bytes 2027520
  79.8 3.5 copy-start.29
  83.3 110.2 %collective-permute-start.1 = (bf16[48,576]{1,0:T(8,128)(2,1)S(1)}, bf16[48,576]{1,0:T(8,128)(2,1)S(1)}, u32[]{:S(2)}, u32[]{:S(2)}) collective-permute-start(bf16[48,576]{1,0:T(8,128)(2,1)S(1)} %pad_maximum_fusion.2), channel_id=1, source_target_pairs={{0,30},{1,31},{2,0},{3,1},{4,2},{5,3},{6,4},{7,5},{8,6},{9,7},{10,... | collective-permute-start | bytes 165896 | tf_op jit(solution)/shard_map/ppermute | solution.py:19
  194.3 5.8 collective-permute-start.2
  200.9 3.9 collective-permute-start.3
  205.6 2.2 copy-start.26
  205.6 14.6 %collective-permute-start.4 = (bf16[384,576]{1,0:T(8,128)(2,1)}, bf16[384,576]{1,0:T(8,128)(2,1)}, u32[]{:S(2)}, u32[]{:S(2)}) collective-permute-start(bf16[384,576]{1,0:T(8,128)(2,1)} %get-tuple-element.284), channel_id=1, source_target_pairs={{0,16},{1,17},{2,18},{3,19},{4,20},{5,21},{6,22},{7,23},{8,24},{9,... | collective-permute-start | bytes 1327112 | tf_op jit(solution)/shard_map/ppermute | solution.py:19
  207.9 6.1 copy-start.21
  220.2 4.2 copy-start.14
  224.3 1.5 copy-start.12
  242.1 6.3 copy-start.28
  278.5 1.6 copy-start
  278.5 1.6 copy-start.27
  278.5 1.6 copy-start.31
  278.9 2.9 copy-start.41
  315.1 5.6 copy-start.1
  315.1 5.6 copy-start.39
  321.5 1.9 copy-start.2
  321.5 1.9 copy-start.30
  323.4 1.6 copy-start.37
  323.4 1.6 copy-start.38
  328.1 1.7 copy-start.3
  328.1 2.5 copy-start.24
  330.0 16.4 %copy-start.22 = (bf16[1024,768]{0,1:T(8,128)(2,1)}, bf16[1024,768]{0,1:T(8,128)(2,1)S(1)}, u32[]{:S(2)}) copy-start(bf16[1024,768]{0,1:T(8,128)(2,1)S(1)} %convert_element_type.126) | copy-start | bytes 4718596
  330.7 15.7 %copy-start.25 = (bf16[768,768]{1,0:T(8,128)(2,1)S(1)}, bf16[768,768]{1,0:T(8,128)(2,1)}, u32[]{:S(2)}) copy-start(bf16[768,768]{1,0:T(8,128)(2,1)} %all-gather.8.cloned.1.call-done) | copy-start | bytes 3538948
  346.4 5.1 copy-start.4
  353.8 3.4 copy-start.43
  355.5 1.7 copy-start.10
  373.7 1.9 copy-start.6
  375.6 3.9 copy-start.5
  386.4 7.1 copy-start.18
  393.5 2.0 copy-start.7
  395.6 1.2 copy-start.19
  396.7 1.1 copy-start.8
  398.2 1.9 copy-start.6
  400.1 4.0 copy-start.5
  410.9 7.1 copy-start.18
  418.0 2.0 copy-start.7
  420.0 1.2 copy-start.19
  421.2 1.1 copy-start.8
  426.8 8.1 copy-start.9
  441.5 1.9 copy-start.20
  443.2 1.5 copy-start.15
  444.6 3.2 copy-start.16
  444.6 3.3 copy-start.23
  447.9 202.6 %reduce-scatter.15.cloned.1.call-start = ((), (), s32[]{:S(2)}) async-start(), calls=%async_computation.9 | async-start | bytes 3244032
  454.6 1.4 copy-start.17
  454.6 299.5 %reduce-scatter.13.cloned.1.call-start = ((), (), s32[]{:S(2)}) async-start(), calls=%async_computation.8 | async-start | bytes 2433024 | tf_op jit(solution)/shard_map/reduce_scatter | solution.py:101
  461.8 5.4 copy-start.34
  461.8 5.4 copy-start.40
  461.8 5.4 copy-start.35
  461.8 397.0 %reduce-scatter.11.cloned.1.call-start = ((), (), s32[]{:S(2)}) async-start(), calls=%async_computation.7 | async-start | bytes 2433024 | tf_op jit(solution)/shard_map/reduce_scatter | solution.py:254
  467.1 3.0 copy-start.42
  467.1 3.0 copy-start.33
  467.1 3.1 copy-start.32
  467.1 3.1 copy-start.36
  467.2 5.1 copy-start.13
  472.3 4.0 copy-start.11
Sparse Core Ops, SparseCore 0:
  10.9 56.8 all-gather.5
  70.7 53.1 all-gather.7
  126.9 54.0 all-gather.9
  448.0 95.8 reduce-scatter.16
  549.8 100.5 reduce-scatter.14
  656.1 97.9 reduce-scatter.12
  760.8 97.9 reduce-scatter.10
